TPU v7x, 128 devices: a whole 4x4x4 slice. The times are simulated.
128 devices in a mesh: row: 16 (over y, x), col: 8 (over z, core).
Axes of the slice: x: 4, y: 4, z: 4, core: 2. Of those that a mesh axis runs over, the one named last changes fastest.
Arguments:
- amplitudes: bfloat16 [16384, 3072], P(('row', 'col')), may hold values from -6 to 6
- integrals: bfloat16 [8, 3072, 9600], P('col', None, 'row'), may hold values from -0.109375 to 0.109375
- irreps: int32 [16384], P(('row', 'col')), may hold values from 0 to 7, as said below
- row_mirror: int32 [16384], P(('row', 'col')), may hold values from 0 to 127, as said below
- col_mirror: int32 [9600], replicated, may hold values from 0 to 9599, as said below
Outputs:
- symmetrized: bfloat16 [16384, 9600], P(('row', 'col'))
Inputs may be any that keep to these rules, and one draw needn't show every extreme that they name: `irreps`: among the 128 pairs of one block, no irrep occurs more than 32 times; in every block one irrep, the same for all blocks, occurs exactly 32 times. A pair and its mirrored partner have the same irrep. `row_mirror`: within each block of 128 pairs the map is an involution without fixed points. `col_mirror`: an involution of the 9600 slab columns without fixed points.
All inputs are finite; a program needn't handle non-finite values.
Results may differ from a plain program's by a relative error of at most 0.0051.
Values may be sent and summed in bfloat16 or wider, within the bound.
A program may use at most 192 MiB of HBM per device.

v0:
```python
import jax
import jax.numpy as jnp
from jax import lax
from jax.sharding import PartitionSpec as P

IRREPS = 8


def body(amplitudes, integrals, irreps, row_mirror, col_mirror):
    pair_count = amplitudes.shape[0]
    contract = amplitudes.shape[1]
    col_count = lax.axis_size("col")
    per_owner = integrals.shape[0]
    capacity = pair_count // 4
    onehot = (irreps[:, None] == jnp.arange(IRREPS, dtype=jnp.int32)[None, :]).astype(jnp.int32)
    before = jnp.cumsum(onehot, axis=0) - onehot
    slot_index = jnp.sum(before * onehot, axis=1)
    owner_col = irreps // per_owner
    within = irreps % per_owner
    position = within * (col_count * capacity) + owner_col * capacity + slot_index
    outgoing = (
        jnp.zeros((per_owner * col_count * capacity, contract), jnp.bfloat16)
        .at[position]
        .set(amplitudes)
    )
    outgoing = outgoing.reshape(per_owner, col_count, capacity, contract)
    arrived = lax.all_to_all(outgoing, "col", split_axis=1, concat_axis=1, tiled=True)
    arrived = arrived.reshape(per_owner, col_count * capacity, contract)
    shares = jnp.einsum(
        "irk,iks->irs",
        lax.all_gather(arrived, "row", axis=1, tiled=True),
        integrals,
        preferred_element_type=jnp.float32,
    ).astype(jnp.bfloat16)
    result = lax.all_to_all(shares, "row", split_axis=1, concat_axis=2, tiled=True)
    slab_width = result.shape[2]
    result = result.reshape(per_owner, col_count, capacity, slab_width)
    returned = lax.all_to_all(result, "col", split_axis=1, concat_axis=1, tiled=True)
    ladder = returned.reshape(per_owner * col_count * capacity, slab_width)[position]
    mirrored = ladder[row_mirror][:, col_mirror]
    return (ladder.astype(jnp.float32) + mirrored.astype(jnp.float32)).astype(jnp.bfloat16)


def solution(mesh):
    return jax.shard_map(
        body,
        mesh=mesh,
        in_specs=(
            P(("row", "col"), None),
            P("col", None, "row"),
            P(("row", "col")),
            P(("row", "col")),
            P(),
        ),
        out_specs=P(("row", "col"), None),
        check_vma=False,
    )
```

profile of v0, /device:TPU:0, one launch (start us, length us, event | category | flops | bytes accessed | tf_op | source)
XLA Modules:
  0.0 592.9 jit_solution(5129053764023563648)
XLA Ops:
  6.5 0.0 all-gather.2.cloned.1.call-start
  6.5 0.7 fusion.12
  7.3 0.2 reduce_window_sum.11
  7.5 0.8 select_reduce_fusion
  8.3 0.7 compare_select_fusion.2
  9.0 2.8 scatter_custom_fusion
  11.8 27.1 %all_to_all.25 = bf16[1,8,32,3072]{3,2,0,1:T(8,128)(2,1)} all-to-all(bf16[1,8,32,3072]{3,2,0,1:T(8,128)(2,1)S(1)} %bitcast.34), channel_id=1, replica_groups=mesh['row'=16,'col'=8] {'col'}, dimensions={1} | all-to-all | bytes 3145728 | tf_op jit(solution)/shard_map/all_to_all | solution.py:27
  38.9 0.0 all-gather.2.cloned.1.call-update
  38.9 153.7 %all-gather.2.cloned.1.call-done = bf16[1,4096,3072]{2,1,0:T(8,128)(2,1)} async-done(((bf16[1,256,3072]{2,1,0:T(8,128)(2,1)}), bf16[1,4096,3072]{2,1,0:T(8,128)(2,1)}) %all-gather.2.cloned.1.call-update) | async-done | bytes 25165840 | tf_op jit(solution)/shard_map/all_gather | solution.py:31
  192.6 22.7 %fusion.5 = bf16[1,4096,600]{1,2,0:T(8,128)(2,1)} fusion(bf16[1,4096,3072]{2,1,0:T(8,128)(2,1)} %all-gather.2.cloned.1.call-done, bf16[1,3072,600]{1,2,0:T(8,128)(2,1)} %param.6), kind=kOutput, calls=%fused_computation.7 | convolution fusion | flops 15101952000 | bytes 33767424 | tf_op jit(solution)/shard_map/irk,iks->irs/dot_general | solution.py:29
  215.3 21.3 %copy.18 = bf16[1,4096,600]{2,0,1:T(2,128)(2,1)} copy(bf16[1,4096,600]{1,2,0:T(8,128)(2,1)} %fusion.5) | data formatting | bytes 9830400 | tf_op jit(solution)/shard_map/convert_element_type | solution.py:34
  236.5 0.5 broadcast.43
  237.1 113.4 %reduce = bf16[4096,600]{1,0:T(8,128)(2,1)} reduce(bf16[4096,1,600]{2,1,0:T(2,128)(2,1)} %bitcast.28, bf16[]{:T(256)} %broadcast.43), dimensions={1}, to_apply=%bitcast.26.reduce_sub_computation | reduce | bytes 9830402
  350.4 14.9 %reshape.67 = bf16[16,2,76800]{2,1,0:T(2,128)(2,1)} reshape(bf16[4096,600]{1,0:T(8,128)(2,1)} %reduce) | data formatting | bytes 9830400
  365.3 64.0 %all_to_all.26 = bf16[16,2,76800]{2,1,0:T(2,128)(2,1)} all-to-all(bf16[16,2,76800]{2,1,0:T(2,128)(2,1)} %reshape.67), channel_id=1, replica_groups=mesh['row'=16,'col'=8] {'row'}, dimensions={0} | all-to-all | bytes 9830400 | tf_op jit(solution)/shard_map/all_to_all | solution.py:35
  429.3 16.1 %reshape.68 = bf16[4096,1,600]{2,1,0:T(2,128)(2,1)} reshape(bf16[16,2,76800]{2,1,0:T(2,128)(2,1)} %all_to_all.26) | data formatting | bytes 9830400
  445.4 7.2 %copy.25 = bf16[1,4096,600]{2,1,0:T(8,128)(2,1)} copy(bf16[1,4096,600]{2,0,1:T(2,128)(2,1)} %bitcast.29) | data formatting | bytes 9830400
  452.6 8.6 %copy.24 = bf16[1,16,256,600]{2,1,3,0:T(8,128)(2,1)} copy(bf16[1,16,256,600]{3,2,1,0:T(8,128)(2,1)} %bitcast.30) | data formatting | bytes 9830400 | tf_op jit(solution)/shard_map/all_to_all | solution.py:35
  461.2 9.5 %copy.20 = bf16[1,256,16,600]{3,2,1,0:T(8,128)(2,1)} copy(bf16[1,256,16,600]{1,2,3,0:T(8,128)(2,1)} %bitcast.32) | data formatting | bytes 9830400 | tf_op jit(solution)/shard_map/all_to_all | solution.py:35
  470.7 9.1 %reshape.26 = bf16[1,8,32,9600]{3,2,1,0:T(8,128)(2,1)} reshape(bf16[1,256,16,600]{3,2,1,0:T(8,128)(2,1)} %copy.20) | data formatting | bytes 9830400 | tf_op jit(solution)/shard_map/reshape | solution.py:37
  479.8 0.0 copy-start.1
  479.8 0.0 copy-start
  479.8 5.0 all-to-all-start.2
  484.8 0.0 copy-done.1
  484.8 0.0 copy-done
  484.9 57.1 %all-to-all-done.2 = bf16[1,8,32,9600]{3,2,0,1:T(8,128)(2,1)} async-done(((bf16[1,8,32,9600]{3,2,0,1:T(8,128)(2,1)}), bf16[1,8,32,9600]{3,2,0,1:T(8,128)(2,1)}, u32[]{:S(2)}, u32[]{:S(2)}) %all-to-all-start.2) | async-done | bytes 4915232 | tf_op jit(solution)/shard_map/all_to_all | solution.py:38
  541.9 7.5 %gather_fusion = bf16[128,9600]{1,0:T(8,128)(2,1)S(1)} fusion(bf16[256,9600]{1,0:T(8,128)(2,1)} %bitcast.8, s32[1024]{0:T(1024)S(1)} %pad_clamp_fusion.2), kind=kCustom, calls=%fused_computation | custom fusion | bytes 4915712 | tf_op jit(solution)/shard_map/gather | solution.py:39
  549.4 3.5 gather_fusion.1
  553.0 4.3 copy.22
  557.3 20.7 %gather_fusion.2 = bf16[9600,128]{1,0:T(8,128)(2,1)} fusion(bf16[128,9600]{0,1:T(8,128)(2,1)} %copy.22, s32[10240]{0:T(1024)S(1)} %pad_clamp_fusion), kind=kCustom, calls=%fused_computation.2 | custom fusion | bytes 4953600 | tf_op jit(solution)/shard_map/gather | solution.py:40
  578.0 4.4 copy.23
  582.3 3.7 fusion.8
  (5 shorter events, 0.0 us)
Async XLA Ops:
  6.5 186.1 %all-gather.2.cloned.1.call-start = ((), (), s32[]{:S(2)}) async-start(), calls=%async_computation.3 | async-start | bytes 26738688 | tf_op jit(solution)/shard_map/all_gather | solution.py:31
  479.8 5.0 copy-start.1
  479.8 5.0 copy-start
  479.8 62.1 %all-to-all-start.2 = ((bf16[1,8,32,9600]{3,2,0,1:T(8,128)(2,1)}), bf16[1,8,32,9600]{3,2,0,1:T(8,128)(2,1)}, u32[]{:S(2)}, u32[]{:S(2)}) async-start(bf16[1,8,32,9600]{3,2,0,1:T(8,128)(2,1)} %bitcast.31), calls=%async_computation.2 | async-start | bytes 9830400 | tf_op jit(solution)/shard_map/all_to_all | solution.py:38
Sparse Core Ops, SparseCore 0:
  39.0 153.5 all-gather.1
where the time goes:
time: 596 us; the launch traced here: 593 us
  waiting for transfers between devices  211 us (35%)
  local copies, waits for them, and re-layouts  130 us (22%)
  other arithmetic  119 us (20%)
  blocking collectives  91.1 us (15%)
  matrix products  22.7 us (4%)
  between operations  13.5 us (2%)
    all_gather x1, waiting for transfers between devices, body(): lax.all_gather(arrived, 'row', axis=1, tiled=True)  154 us
    unnamed x1, other arithmetic  113 us
    all_to_all x1, blocking collectives, body(): lax.all_to_all(shares, 'row', split_axis=1, concat_axis=2, tiled=True)  64 us
    all_to_all x1, waiting for transfers between devices, body(): lax.all_to_all(result, 'col', split_axis=1, concat_axis=1, tiled=True)  57.1 us
    unnamed x8, local copies, waits for them, and re-layouts  38.7 us
    gather x4, local copies, waits for them, and re-layouts, body(): mirrored = ladder[row_mirror][:, col_mirror]  32.9 us
    all_to_all x1, blocking collectives, body(): lax.all_to_all(outgoing, 'col', split_axis=1, concat_axis=1, tiled=True)  27.1 us
    dot_general x1, matrix products, body(): jnp.einsum('irk,iks->irs', lax.all_gather(arrived, 'row', axis=1, tiled=T...  22.7 us
  transfers between devices with their start and end apart: 2, of which 2 were waited for; matrix products, arithmetic and copies ran while one was open for 0% of the time, Pallas kernels for 0%

commit v1 on v0

v1 whole, which is shorter than its diff:
```python
import functools

import jax
import jax.numpy as jnp
from jax import lax
from jax.experimental import pallas as pl
from jax.experimental.pallas import tpu as pltpu
from jax.sharding import PartitionSpec as P

IRREPS = 8
KW = 3072
HALF = KW // 2
ROWS = 128
CAP = 32
SLOTS = IRREPS * CAP
COLS = 600
SLAB = 9600
NB = 16
NC = 5
CH = COLS // NC
MESH = pl.DeviceIdType.MESH
BF = jnp.bfloat16
F32 = jnp.float32


def ladder_kernel(
    amp_ref, w_ref, irr_ref,
    t_ref, a_all, w_all,
    xbuf, wbuf, abuf, pbuf, ys, tbuf, pos,
    ws, wr, rs, rr, ps, pr, ts, tr, ls, al, wl,
):
    row = lax.axis_index("row")
    col = lax.axis_index("col")
    y = row // 4
    x = row % 4
    z = col // 2
    core = col % 2

    def plane(dx, dy):
        return {"row": ((y + dy) % 4) * 4 + (x + dx) % 4, "col": col}

    def line(dz):
        return {"row": row, "col": ((z + dz) % 4) * 2 + core}

    sibling = {"row": row, "col": z * 2 + (1 - core)}

    def remote(src, dst, send, recv, where):
        return pltpu.make_async_remote_copy(
            src_ref=src, dst_ref=dst, send_sem=send, recv_sem=recv, device_id=where, device_id_type=MESH
        )

    def zop(j, name):
        rows = pl.ds(pl.multiple_of(j * CH, 8), CH)
        if name == "plus":
            return remote(w_ref.at[rows], w_all.at[4, rows], ws.at[j, 4], wr.at[j, 4], line(1))
        if name == "minus":
            return remote(w_ref.at[rows], w_all.at[2, rows], ws.at[j, 2], wr.at[j, 2], line(3))
        if name == "far0":
            k = pl.ds(0, HALF)
            return remote(w_all.at[4, rows, k], w_all.at[6, rows, k], ws.at[j, 6], wr.at[j, 6], line(1))
        if name == "far1":
            k = pl.ds(HALF, HALF)
            return remote(w_all.at[2, rows, k], w_all.at[6, rows, k], ws.at[j, 0], wr.at[j, 0], line(3))
        slot = {"sib2": 2, "sib4": 4, "sib6": 6}[name]
        return remote(
            w_all.at[slot, rows], w_all.at[slot + 1, rows], ws.at[j, slot + 1], wr.at[j, slot + 1], sibling
        )

    def sibown():
        return remote(w_ref, w_all.at[1], ws.at[0, 1], wr.at[0, 1], sibling)

    def slot(h, d1, d2):
        return d2 * 4 + d1 if h == 0 else d1 * 4 + d2

    def rop(h, phase, n):
        d1 = 0 if phase == 4 else phase
        if phase == 4:
            place = lambda d: slot(h, d, 0)
            to = lambda s: plane(s, 0) if h == 0 else plane(0, s)
        else:
            place = lambda d: slot(h, d1, d)
            to = lambda s: plane(0, s) if h == 0 else plane(s, 0)
        full, first, second = pl.ds(64 * h, 64), pl.ds(64 * h, 32), pl.ds(64 * h + 32, 32)
        source, target, part, way = (
            (0, 3, full, 1), (0, 1, full, 3), (3, 2, first, 1), (1, 2, second, 3)
        )[n]
        k = place(source)
        src = amp_ref.at[part] if k == 0 else a_all.at[k, part]
        return remote(
            src, a_all.at[place(target), part], rs.at[h, phase, n], rr.at[h, phase, n], to(way)
        )

    def pop(k):
        dx, dy = k % 4, k // 4
        there = ((4 - dy) % 4) * 4 + (4 - dx) % 4
        return remote(pos.at[0], pos.at[there], ps.at[there], pr.at[there], plane(dx, dy))

    def top(j, k):
        rows = pl.ds(pl.multiple_of(row * COLS + j * CH, 8), CH)
        return remote(tbuf.at[j, k], t_ref.at[rows], ts.at[j], tr.at[j], plane(k % 4, k // 4))

    barrier = pltpu.get_barrier_semaphore()

    def greet(k, c):
        pl.semaphore_signal(barrier, inc=1, device_id=plane(k % 4, k // 4), device_id_type=MESH)
        return c

    lax.fori_loop(1, NB, greet, 0)
    for where in (line(1), line(3), sibling):
        pl.semaphore_signal(barrier, inc=1, device_id=where, device_id_type=MESH)
    pl.semaphore_wait(barrier, NB + 2)

    for j in range(2):
        zop(j, "plus").start()
        zop(j, "minus").start()
    for phase in (4, 0):
        for h in range(2):
            rop(h, phase, 0).start()
            rop(h, phase, 1).start()
    sibown().start()
    own_w = pltpu.make_async_copy(w_ref, w_all.at[0], ls.at[NC])
    own_w.start()
    own_a = pltpu.make_async_copy(amp_ref, a_all.at[0], ls.at[NC + 1])
    own_a.start()

    irr = irr_ref[...]
    onehot = (lax.broadcasted_iota(jnp.int32, (IRREPS, ROWS), 0) == irr).astype(F32)
    earlier = (
        lax.broadcasted_iota(jnp.int32, (ROWS, ROWS), 0) < lax.broadcasted_iota(jnp.int32, (ROWS, ROWS), 1)
    ).astype(F32)
    before = jnp.dot(onehot.astype(BF), earlier.astype(BF), preferred_element_type=F32)
    rank = jnp.sum(before * onehot, axis=0, keepdims=True)
    place = irr.astype(F32) * CAP + rank
    pos[0] = jnp.broadcast_to(place, (8, ROWS))

    def send_pos(k, c):
        pop(k).start()
        return c

    lax.fori_loop(1, NB, send_pos, 0)

    def pass_on(j):
        zop(j, "plus").wait_recv()
        zop(j, "far0").start()
        zop(j, "sib4").start()
        zop(j, "minus").wait_recv()
        zop(j, "far1").start()
        zop(j, "sib2").start()

    def own_chunk(j):
        zop(j, "plus").start()
        zop(j, "minus").start()

    def ring_pass(phase):
        for h in range(2):
            rop(h, phase, 0).wait_recv()
            rop(h, phase, 2).start()
            rop(h, phase, 1).wait_recv()
            rop(h, phase, 3).start()

    def ring_send(phase):
        for h in range(2):
            rop(h, phase, 0).start()
            rop(h, phase, 1).start()

    ring_pass(4)
    ring_send(3)
    ring_send(1)
    for h in range(2):
        rop(h, 4, 2).wait_recv()
        rop(h, 4, 3).wait_recv()
    ring_send(2)
    ring_pass(0)
    pass_on(0)
    own_chunk(2)
    ring_pass(3)
    ring_pass(1)
    pass_on(1)
    own_chunk(3)
    ring_pass(2)
    for phase in (0, 3, 1, 2):
        for h in range(2):
            rop(h, phase, 2).wait_recv()
            rop(h, phase, 3).wait_recv()
    own_a.wait()
    own_w.wait()

    def wait_pos(k, c):
        pop(k).wait_recv()
        return c

    lax.fori_loop(1, NB, wait_pos, 0)

    def aload(k, buf):
        return pltpu.make_async_copy(a_all.at[k], abuf.at[buf], al.at[buf])

    aload(0, 0).start()

    def sort_block(k, c):
        buf = k % 2

        @pl.when(k + 1 < NB)
        def _():
            aload(k + 1, 1 - buf).start()

        hot = (
            lax.broadcasted_iota(jnp.int32, (SLOTS, ROWS), 0).astype(F32) == pos[k][0:1, :]
        ).astype(F32).astype(BF)
        pbuf[k] = hot
        aload(k, buf).wait()
        for n in range(6):
            lanes = pl.ds(n * 512, 512)
            got = jnp.dot(hot, abuf[buf, :, lanes], preferred_element_type=F32).astype(BF)
            xbuf[:, pl.ds(pl.multiple_of(k * CAP, CAP), CAP), lanes] = got.reshape(IRREPS, CAP, 512)
        return c

    lax.fori_loop(0, NB, sort_block, 0)

    def wload(j, n):
        rows = pl.ds(pl.multiple_of(j * CH, 8), CH)
        return pltpu.make_async_copy(w_all.at[n, rows], wbuf.at[n], wl.at[n])

    def chunk(j, c):
        @pl.when(j + 2 < NC)
        def _():
            pass_on(j + 2)

        @pl.when(j + 4 < NC)
        def _():
            own_chunk(j + 4)

        @pl.when(j == 0)
        def _():
            sibown().wait_recv()

        zop(j, "sib2").wait_recv()
        zop(j, "sib4").wait_recv()
        for n in range(6):
            wload(j, n).start()

        def irrep(n, c):
            @pl.when(n == 5)
            def _():
                zop(j, "far0").wait_recv()
                zop(j, "far1").wait_recv()
                zop(j, "sib6").start()
                wload(j, 6).start()

            @pl.when(n == 7)
            def _():
                zop(j, "sib6").wait_recv()
                wload(j, 7).start()

            m = n // 2
            dz = m + m // 2 - 2 * (m // 3)
            which = 2 * ((z + dz) % 4) + (core + n % 2) % 2
            wload(j, n).wait()
            got = lax.dot_general(
                xbuf[which], wbuf[n], (((1,), (1,)), ((), ())), preferred_element_type=F32
            ).astype(BF)
            ys[:, pl.ds(pl.multiple_of(which * CAP, CAP), CAP), 0:CH] = got.reshape(NB, CAP, CH)
            return c

        lax.fori_loop(0, IRREPS, irrep, 0)

        def back(k, c):
            tbuf[j, k] = lax.dot_general(
                ys[k], pbuf[k], (((0,), (0,)), ((), ())), preferred_element_type=F32
            )[0:CH].astype(BF)

            @pl.when(k > 0)
            def _():
                top(j, k).start()

            return c

        lax.fori_loop(0, NB, back, 0)
        rows = pl.ds(pl.multiple_of(row * COLS + j * CH, 8), CH)
        pltpu.make_async_copy(tbuf.at[j, 0], t_ref.at[rows], ls.at[j]).start()
        return c

    lax.fori_loop(0, NC, chunk, 0)

    def finish(j, c):
        rows = pl.ds(pl.multiple_of(row * COLS + j * CH, 8), CH)
        pltpu.make_async_copy(tbuf.at[j, 0], t_ref.at[rows], ls.at[j]).wait()
        some = t_ref.at[pl.ds(0, (NB - 1) * CH)]
        pltpu.make_async_copy(some, some, ts.at[j]).wait()
        pltpu.make_async_copy(some, some, tr.at[j]).wait()
        for name in ("plus", "minus", "far0", "far1", "sib2", "sib4", "sib6"):
            zop(j, name).wait_send()
        return c

    lax.fori_loop(0, NC, finish, 0)
    sibown().wait_send()
    for phase in range(5):
        for h in range(2):
            for n in range(4):
                rop(h, phase, n).wait_send()

    def done_pos(k, c):
        pop(k).wait_send()
        return c

    lax.fori_loop(1, NB, done_pos, 0)


def ladder(amplitudes, integrals, irreps):
    dma = pltpu.SemaphoreType.DMA
    hbm = pl.BlockSpec(memory_space=pl.ANY)
    t, _, _ = pl.pallas_call(
        ladder_kernel,
        out_shape=(
            jax.ShapeDtypeStruct((SLAB, ROWS), BF),
            jax.ShapeDtypeStruct((NB, ROWS, KW), BF),
            jax.ShapeDtypeStruct((IRREPS, COLS, KW), BF),
        ),
        in_specs=[hbm, hbm, pl.BlockSpec(memory_space=pltpu.VMEM)],
        out_specs=(hbm, hbm, hbm),
        scratch_shapes=[
            pltpu.VMEM((IRREPS, NB * CAP, KW), BF),
            pltpu.VMEM((IRREPS, CH, KW), BF),
            pltpu.VMEM((2, ROWS, KW), BF),
            pltpu.VMEM((NB, SLOTS, ROWS), BF),
            pltpu.VMEM((NB, SLOTS, 128), BF),
            pltpu.VMEM((NC, NB, CH, ROWS), BF),
            pltpu.VMEM((NB, 8, ROWS), F32),
            dma((NC, 8)),
            dma((NC, 8)),
            dma((2, 5, 4)),
            dma((2, 5, 4)),
            dma((NB,)),
            dma((NB,)),
            dma((NC,)),
            dma((NC,)),
            dma((NC + 2,)),
            dma((2,)),
            dma((8,)),
        ],
        compiler_params=pltpu.CompilerParams(
            collective_id=0, has_side_effects=True, vmem_limit_bytes=56 * 1024 * 1024
        ),
        name="ladder",
    )(amplitudes, integrals, irreps)
    return t


GB = 384
NG = SLAB // GB
UNROLL = 16


def mirror_kernel(col_ref, t_ref, row_ref, out_ref, tf, g):
    def widen(i, c):
        rows = pl.ds(pl.multiple_of(i * GB, GB), GB)
        tf[rows, :] = t_ref[rows, :].astype(F32)
        return c

    lax.fori_loop(0, NG, widen, 0)
    lane = lax.broadcasted_iota(jnp.int32, (ROWS, ROWS), 1)
    sub = lax.broadcasted_iota(jnp.int32, (ROWS, ROWS), 0)
    same = (lane == sub).astype(F32).astype(BF)
    swap = (sub == row_ref[...]).astype(F32).astype(BF)

    def block(i, c):
        base = pl.multiple_of(i * GB, GB)

        def pick(u, c):
            for r in range(UNROLL):
                at = u * UNROLL + r
                g[pl.ds(at, 1), :] = tf[pl.ds(col_ref[base + at], 1), :]
            return c

        lax.fori_loop(0, GB // UNROLL, pick, 0)
        nt = (((1,), (1,)), ((), ()))
        here = lax.dot_general(same, t_ref[pl.ds(base, GB), :], nt, preferred_element_type=F32)
        there = lax.dot_general(swap, g[...].astype(BF), nt, preferred_element_type=F32)
        out_ref[:, pl.ds(base, GB)] = (here + there).astype(BF)
        return c

    lax.fori_loop(0, NG, block, 0)


def mirror(t, row_mirror, col_mirror):
    vmem = pl.BlockSpec(memory_space=pltpu.VMEM)
    return pl.pallas_call(
        mirror_kernel,
        out_shape=jax.ShapeDtypeStruct((ROWS, SLAB), BF),
        in_specs=[pl.BlockSpec(memory_space=pltpu.SMEM), vmem, vmem],
        out_specs=vmem,
        scratch_shapes=[pltpu.VMEM((SLAB, ROWS), F32), pltpu.VMEM((GB, ROWS), F32)],
        compiler_params=pltpu.CompilerParams(vmem_limit_bytes=32 * 1024 * 1024),
        name="mirror",
    )(col_mirror, t, row_mirror)


def body(amplitudes, integrals, irreps, row_mirror, col_mirror):
    w = jnp.swapaxes(integrals[0], 0, 1)
    t = ladder(amplitudes, w, irreps.reshape(1, ROWS))
    return mirror(t, row_mirror.reshape(1, ROWS), col_mirror)


def solution(mesh):
    return jax.shard_map(
        body,
        mesh=mesh,
        in_specs=(
            P(("row", "col"), None),
            P("col", None, "row"),
            P(("row", "col")),
            P(("row", "col")),
            P(),
        ),
        out_specs=P(("row", "col"), None),
        check_vma=False,
    )
```

time: 596 us -> 262 us (0.44)
  Pallas kernels: 0 us -> 258 us
  waiting for transfers between devices: 211 us -> 0 us
  local copies, waits for them, and re-layouts: 130 us -> 1.69 us
  other arithmetic: 119 us -> 0 us
  blocking collectives: 91.1 us -> 0 us
  matrix products: 22.7 us -> 0 us
  between operations: 13.5 us -> 0.03 us
    pallas_call x0 -> x2, Pallas kernels: none -> 258 us  [the longest x1 237 us: ladder(): pl.pallas_call(ladder_kernel, out_shape=(jax.ShapeDtypeStruct((SLAB, ROWS...]
    all_gather x1 -> x0, waiting for transfers between devices: 154 us -> none  [body(): lax.all_gather(arrived, 'row', axis=1, tiled=True)]
    unnamed x1 -> x0, other arithmetic: 113 us -> none
    all_to_all x2 -> x0, blocking collectives: 91.1 us -> none  [the longest x1 64 us: body(): lax.all_to_all(shares, 'row', split_axis=1, concat_axis=2, tiled=True)]
    all_to_all x1 -> x0, waiting for transfers between devices: 57.1 us -> none  [body(): lax.all_to_all(result, 'col', split_axis=1, concat_axis=1, tiled=True)]
    gather x5 -> x0, local copies, waits for them, and re-layouts: 40.4 us -> none  [the longest x4 32.9 us: body(): mirrored = ladder[row_mirror][:, col_mirror]]
    unnamed x8 -> x6, local copies, waits for them, and re-layouts: 38.7 us -> 1.69 us
    dot_general x1 -> x0, matrix products: 22.7 us -> none  [body(): jnp.einsum('irk,iks->irs', lax.all_gather(arrived, 'row', axis=1, tiled=T...]
  transfers between devices with their start and end apart: 2 -> 0, of which waited for: 2 -> 0; matrix products, arithmetic and copies ran while one was open for 0% -> 0% of each run, Pallas kernels for 0% -> 0%
where the time goes in v1:
time: 262 us; the launch traced here: 260 us
  Pallas kernels  258 us (98%)
    pallas_call x1, Pallas kernels, ladder(): pl.pallas_call(ladder_kernel, out_shape=(jax.ShapeDtypeStruct((SLAB, ROWS...  237 us
    pallas_call x1, Pallas kernels, mirror(): pl.pallas_call(mirror_kernel, out_shape=jax.ShapeDtypeStruct((ROWS, SLAB)...  21.2 us

profile of v1, /device:TPU:0, one launch (start us, length us, event | category | flops | bytes accessed | tf_op | source)
XLA Modules:
  0.0 260.2 jit_solution(3659496618772001977)
XLA Ops:
  0.0 0.0 copy-start.1
  0.0 0.0 copy-start.2
  0.0 237.2 %ladder.1 = (bf16[9600,128]{1,0:T(8,128)(2,1)}, bf16[16,128,3072]{2,1,0:T(8,128)(2,1)}, bf16[8,600,3072]{2,1,0:T(8,128)(2,1)}) custom-call(bf16[128,3072]{1,0:T(8,128)(2,1)} %amp_ref.1, bf16[600,3072]{1,0:T(8,128)(2,1)} %bitcast.6, s32[1,128]{1,0:T(1,128)} %bitcast.7), custom_call_target="tpu_custom_call" | custom-call | tf_op jit(solution)/shard_map/ladder/pallas_call | solution.py:311
  237.2 0.0 copy-done.1
  237.2 0.0 copy-done.2
  237.2 0.0 copy-start
  237.3 1.7 copy-done
  238.9 21.2 %mirror.1 = bf16[128,9600]{1,0:T(8,128)(2,1)} custom-call(s32[9600]{0:T(1024)S(1)} %copy-done.1, bf16[9600,128]{1,0:T(8,128)(2,1)S(1)} %copy-done, s32[1,128]{1,0:T(1,128)S(1)} %bitcast.5), custom_call_target="tpu_custom_call" | custom-call | tf_op jit(solution)/shard_map/mirror/pallas_call | solution.py:386
Async XLA Ops:
  0.0 237.2 %copy-start.1 = (s32[9600]{0:T(1024)S(1)}, s32[9600]{0:T(1024)}, u32[]{:S(2)}) copy-start(s32[9600]{0:T(1024)} %col_ref.1) | copy-start | bytes 115204
  0.0 237.2 %copy-start.2 = (s32[128]{0:T(128)S(1)}, s32[128]{0:T(128)}, u32[]{:S(2)}) copy-start(s32[128]{0:T(128)} %param.8) | copy-start | bytes 1540
  237.2 1.7 copy-start

commit v2 on v1

--- a/solution.py
+++ b/solution.py
@@ -16,8 +16,14 @@
 COLS = 600
 SLAB = 9600
 NB = 16
-NC = 5
-CH = COLS // NC
+PIECES = (128, 128, 128, 128, 48, 40)
+STARTS = (0, 128, 256, 384, 512, 560)
+NP = len(PIECES)
+CHUNKS = ((0, 1), (2, 3), (4, 5))
+NC = len(CHUNKS)
+WIDE = 256
+NARROW = 88
+ABUFS = 4
 MESH = pl.DeviceIdType.MESH
 BF = jnp.bfloat16
 F32 = jnp.float32
@@ -26,7 +32,7 @@
 def ladder_kernel(
     amp_ref, w_ref, irr_ref,
     t_ref, a_all, w_all,
-    xbuf, wbuf, abuf, pbuf, ys, tbuf, pos,
+    xbuf, wbuf, wlast, abuf, pbuf, ys, ylast, tbuf, tlast, pos,
     ws, wr, rs, rr, ps, pr, ts, tr, ls, al, wl,
 ):
     row = lax.axis_index("row")
@@ -50,7 +56,7 @@
         )
 
     def zop(j, name):
-        rows = pl.ds(pl.multiple_of(j * CH, 8), CH)
+        rows = pl.ds(STARTS[j], PIECES[j])
         if name == "plus":
             return remote(w_ref.at[rows], w_all.at[4, rows], ws.at[j, 4], wr.at[j, 4], line(1))
         if name == "minus":
@@ -95,9 +101,20 @@
         there = ((4 - dy) % 4) * 4 + (4 - dx) % 4
         return remote(pos.at[0], pos.at[there], ps.at[there], pr.at[there], plane(dx, dy))
 
-    def top(j, k):
-        rows = pl.ds(pl.multiple_of(row * COLS + j * CH, 8), CH)
-        return remote(tbuf.at[j, k], t_ref.at[rows], ts.at[j], tr.at[j], plane(k % 4, k // 4))
+    def width(c):
+        return sum(PIECES[j] for j in CHUNKS[c])
+
+    def out_rows(c):
+        return pl.ds(pl.multiple_of(row * COLS + STARTS[CHUNKS[c][0]], 8), width(c))
+
+    def staged(c, k):
+        return tbuf.at[c, k, pl.ds(0, width(c))] if c < NC - 1 else tlast.at[k]
+
+    def top(c, k):
+        return remote(staged(c, k), t_ref.at[out_rows(c)], ts.at[c], tr.at[c], plane(k % 4, k // 4))
+
+    def keep(c):
+        return pltpu.make_async_copy(staged(c, 0), t_ref.at[out_rows(c)], ls.at[c])
 
     barrier = pltpu.get_barrier_semaphore()
 
@@ -118,10 +135,6 @@
             rop(h, phase, 0).start()
             rop(h, phase, 1).start()
     sibown().start()
-    own_w = pltpu.make_async_copy(w_ref, w_all.at[0], ls.at[NC])
-    own_w.start()
-    own_a = pltpu.make_async_copy(amp_ref, a_all.at[0], ls.at[NC + 1])
-    own_a.start()
 
     irr = irr_ref[...]
     onehot = (lax.broadcasted_iota(jnp.int32, (IRREPS, ROWS), 0) == irr).astype(F32)
@@ -178,12 +191,11 @@
     pass_on(1)
     own_chunk(3)
     ring_pass(2)
+    pass_on(2)
     for phase in (0, 3, 1, 2):
         for h in range(2):
             rop(h, phase, 2).wait_recv()
             rop(h, phase, 3).wait_recv()
-    own_a.wait()
-    own_w.wait()
 
     def wait_pos(k, c):
         pop(k).wait_recv()
@@ -191,107 +203,141 @@
 
     lax.fori_loop(1, NB, wait_pos, 0)
 
-    def aload(k, buf):
-        return pltpu.make_async_copy(a_all.at[k], abuf.at[buf], al.at[buf])
-
-    aload(0, 0).start()
+    def wload(j, n):
+        if j < CHUNKS[-1][0]:
+            there = wbuf.at[n, pl.ds(128 * (j % 2), PIECES[j])]
+        else:
+            there = wlast.at[n, pl.ds(STARTS[j] - STARTS[CHUNKS[-1][0]], PIECES[j])]
+        src = w_ref if n == 0 else w_all.at[n]
+        return pltpu.make_async_copy(src.at[pl.ds(STARTS[j], PIECES[j])], there, wl.at[j, n])
+
+    def near(c):
+        for j in CHUNKS[c]:
+            if j == 0:
+                sibown().wait_recv()
+            zop(j, "sib2").wait_recv()
+            zop(j, "sib4").wait_recv()
+            for n in range(6):
+                wload(j, n).start()
+
+    def far(c):
+        for j in CHUNKS[c]:
+            zop(j, "far0").wait_recv()
+            zop(j, "far1").wait_recv()
+            zop(j, "sib6").start()
+            wload(j, 6).start()
+        for j in CHUNKS[c]:
+            zop(j, "sib6").wait_recv()
+            wload(j, 7).start()
+
+    def aload(k):
+        return pltpu.make_async_copy(a_all.at[k], abuf.at[k % ABUFS], al.at[k % ABUFS])
 
     def sort_block(k, c):
-        buf = k % 2
-
-        @pl.when(k + 1 < NB)
-        def _():
-            aload(k + 1, 1 - buf).start()
-
         hot = (
             lax.broadcasted_iota(jnp.int32, (SLOTS, ROWS), 0).astype(F32) == pos[k][0:1, :]
         ).astype(F32).astype(BF)
         pbuf[k] = hot
-        aload(k, buf).wait()
+        aload(k).wait()
         for n in range(6):
             lanes = pl.ds(n * 512, 512)
-            got = jnp.dot(hot, abuf[buf, :, lanes], preferred_element_type=F32).astype(BF)
+            got = jnp.dot(hot, abuf[k % ABUFS, :, lanes], preferred_element_type=F32).astype(BF)
             xbuf[:, pl.ds(pl.multiple_of(k * CAP, CAP), CAP), lanes] = got.reshape(IRREPS, CAP, 512)
-        return c
-
-    lax.fori_loop(0, NB, sort_block, 0)
-
-    def wload(j, n):
-        rows = pl.ds(pl.multiple_of(j * CH, 8), CH)
-        return pltpu.make_async_copy(w_all.at[n, rows], wbuf.at[n], wl.at[n])
-
-    def chunk(j, c):
-        @pl.when(j + 2 < NC)
+
+        @pl.when(k + ABUFS < NB)
         def _():
-            pass_on(j + 2)
-
-        @pl.when(j + 4 < NC)
-        def _():
-            own_chunk(j + 4)
-
-        @pl.when(j == 0)
-        def _():
-            sibown().wait_recv()
-
-        zop(j, "sib2").wait_recv()
-        zop(j, "sib4").wait_recv()
-        for n in range(6):
-            wload(j, n).start()
-
-        def irrep(n, c):
-            @pl.when(n == 5)
-            def _():
-                zop(j, "far0").wait_recv()
-                zop(j, "far1").wait_recv()
-                zop(j, "sib6").start()
-                wload(j, 6).start()
-
-            @pl.when(n == 7)
-            def _():
-                zop(j, "sib6").wait_recv()
-                wload(j, 7).start()
-
+            aload(k + ABUFS).start()
+
+        return c
+
+    def multiply(c, first, last):
+        last_chunk = c == NC - 1
+
+        def irrep(n, carry):
             m = n // 2
             dz = m + m // 2 - 2 * (m // 3)
             which = 2 * ((z + dz) % 4) + (core + n % 2) % 2
-            wload(j, n).wait()
             got = lax.dot_general(
-                xbuf[which], wbuf[n], (((1,), (1,)), ((), ())), preferred_element_type=F32
+                xbuf[which],
+                wlast[n] if last_chunk else wbuf[n],
+                (((1,), (1,)), ((), ())),
+                preferred_element_type=F32,
             ).astype(BF)
-            ys[:, pl.ds(pl.multiple_of(which * CAP, CAP), CAP), 0:CH] = got.reshape(NB, CAP, CH)
-            return c
-
-        lax.fori_loop(0, IRREPS, irrep, 0)
-
-        def back(k, c):
-            tbuf[j, k] = lax.dot_general(
-                ys[k], pbuf[k], (((0,), (0,)), ((), ())), preferred_element_type=F32
-            )[0:CH].astype(BF)
-
-            @pl.when(k > 0)
-            def _():
-                top(j, k).start()
-
-            return c
-
-        lax.fori_loop(0, NB, back, 0)
-        rows = pl.ds(pl.multiple_of(row * COLS + j * CH, 8), CH)
-        pltpu.make_async_copy(tbuf.at[j, 0], t_ref.at[rows], ls.at[j]).start()
-        return c
-
-    lax.fori_loop(0, NC, chunk, 0)
-
-    def finish(j, c):
-        rows = pl.ds(pl.multiple_of(row * COLS + j * CH, 8), CH)
-        pltpu.make_async_copy(tbuf.at[j, 0], t_ref.at[rows], ls.at[j]).wait()
-        some = t_ref.at[pl.ds(0, (NB - 1) * CH)]
-        pltpu.make_async_copy(some, some, ts.at[j]).wait()
-        pltpu.make_async_copy(some, some, tr.at[j]).wait()
+            at = pl.ds(pl.multiple_of(which * CAP, CAP), CAP)
+            if last_chunk:
+                ylast[:, at, 0:NARROW] = got.reshape(NB, CAP, NARROW)
+            else:
+                ys[:, at, :] = got.reshape(NB, CAP, WIDE)
+            return carry
+
+        for j in CHUNKS[c]:
+            for n in range(first, last):
+                wload(j, n).wait()
+        lax.fori_loop(first, last, irrep, 0)
+
+    def give_back(c):
+        last_chunk = c == NC - 1
+
+        def back(u, carry):
+            for v in range(4):
+                k = 4 * u + v
+                got = lax.dot_general(
+                    ylast[k] if last_chunk else ys[k],
+                    pbuf[k],
+                    (((0,), (0,)), ((), ())),
+                    preferred_element_type=F32,
+                ).astype(BF)
+                if last_chunk:
+                    tlast[k] = got[0:NARROW]
+                else:
+                    tbuf[c, k] = got
+            for v in range(4):
+                if v == 0:
+
+                    @pl.when(u > 0)
+                    def _():
+                        top(c, 4 * u).start()
+
+                else:
+                    top(c, 4 * u + v).start()
+            return carry
+
+        lax.fori_loop(0, NB // 4, back, 0)
+        keep(c).start()
+
+    pltpu.make_async_copy(amp_ref, abuf.at[0], al.at[0]).start()
+    for k in range(1, ABUFS):
+        aload(k).start()
+    near(0)
+    lax.fori_loop(0, NB, sort_block, 0)
+    pass_on(3)
+    own_chunk(4)
+    own_chunk(5)
+    multiply(0, 0, 6)
+    far(0)
+    multiply(0, 6, 8)
+    near(1)
+    give_back(0)
+    multiply(1, 0, 6)
+    far(1)
+    multiply(1, 6, 8)
+    give_back(1)
+    pass_on(4)
+    pass_on(5)
+    near(2)
+    multiply(2, 0, 6)
+    far(2)
+    multiply(2, 6, 8)
+    give_back(2)
+
+    for c in range(NC):
+        keep(c).wait()
+        some = t_ref.at[pl.ds(0, (NB - 1) * width(c))]
+        pltpu.make_async_copy(some, some, ts.at[c]).wait()
+        pltpu.make_async_copy(some, some, tr.at[c]).wait()
+    for j in range(NP):
         for name in ("plus", "minus", "far0", "far1", "sib2", "sib4", "sib6"):
             zop(j, name).wait_send()
-        return c
-
-    lax.fori_loop(0, NC, finish, 0)
     sibown().wait_send()
     for phase in range(5):
         for h in range(2):
@@ -319,26 +365,29 @@
         out_specs=(hbm, hbm, hbm),
         scratch_shapes=[
             pltpu.VMEM((IRREPS, NB * CAP, KW), BF),
-            pltpu.VMEM((IRREPS, CH, KW), BF),
-            pltpu.VMEM((2, ROWS, KW), BF),
+            pltpu.VMEM((IRREPS, WIDE, KW), BF),
+            pltpu.VMEM((IRREPS, NARROW, KW), BF),
+            pltpu.VMEM((ABUFS, ROWS, KW), BF),
             pltpu.VMEM((NB, SLOTS, ROWS), BF),
+            pltpu.VMEM((NB, SLOTS, WIDE), BF),
             pltpu.VMEM((NB, SLOTS, 128), BF),
-            pltpu.VMEM((NC, NB, CH, ROWS), BF),
+            pltpu.VMEM((NC - 1, NB, WIDE, ROWS), BF),
+            pltpu.VMEM((NB, NARROW, ROWS), BF),
             pltpu.VMEM((NB, 8, ROWS), F32),
-            dma((NC, 8)),
-            dma((NC, 8)),
+            dma((NP, 8)),
+            dma((NP, 8)),
             dma((2, 5, 4)),
             dma((2, 5, 4)),
             dma((NB,)),
             dma((NB,)),
             dma((NC,)),
             dma((NC,)),
-            dma((NC + 2,)),
-            dma((2,)),
-            dma((8,)),
+            dma((NC,)),
+            dma((ABUFS,)),
+            dma((NP, 8)),
         ],
         compiler_params=pltpu.CompilerParams(
-            collective_id=0, has_side_effects=True, vmem_limit_bytes=56 * 1024 * 1024
+            collective_id=0, has_side_effects=True, vmem_limit_bytes=60 * 1024 * 1024
         ),
         name="ladder",
     )(amplitudes, integrals, irreps)
@@ -347,10 +396,10 @@
 
 GB = 384
 NG = SLAB // GB
-UNROLL = 16
-
-
-def mirror_kernel(col_ref, t_ref, row_ref, out_ref, tf, g):
+NT = (((1,), (1,)), ((), ()))
+
+
+def mirror_kernel(col_ref, t_ref, row_ref, out_ref, tf, even, odd):
     def widen(i, c):
         rows = pl.ds(pl.multiple_of(i * GB, GB), GB)
         tf[rows, :] = t_ref[rows, :].astype(F32)
@@ -362,23 +411,30 @@
     same = (lane == sub).astype(F32).astype(BF)
     swap = (sub == row_ref[...]).astype(F32).astype(BF)
 
-    def block(i, c):
-        base = pl.multiple_of(i * GB, GB)
-
-        def pick(u, c):
-            for r in range(UNROLL):
-                at = u * UNROLL + r
-                g[pl.ds(at, 1), :] = tf[pl.ds(col_ref[base + at], 1), :]
-            return c
-
-        lax.fori_loop(0, GB // UNROLL, pick, 0)
-        nt = (((1,), (1,)), ((), ()))
-        here = lax.dot_general(same, t_ref[pl.ds(base, GB), :], nt, preferred_element_type=F32)
-        there = lax.dot_general(swap, g[...].astype(BF), nt, preferred_element_type=F32)
+    def pick(base, g):
+        for q in range(GB // 8):
+            some = [tf[pl.ds(col_ref[base + 8 * q + r], 1), :] for r in range(8)]
+            g[8 * q : 8 * q + 8, :] = jnp.concatenate(some, axis=0)
+
+    def add(base, g):
+        here = lax.dot_general(same, t_ref[pl.ds(base, GB), :], NT, preferred_element_type=F32)
+        there = lax.dot_general(swap, g[...].astype(BF), NT, preferred_element_type=F32)
         out_ref[:, pl.ds(base, GB)] = (here + there).astype(BF)
-        return c
-
-    lax.fori_loop(0, NG, block, 0)
+
+    pick(0, even)
+
+    def two(i, c):
+        first = pl.multiple_of(2 * i * GB, GB)
+        second = pl.multiple_of(first + GB, GB)
+        third = pl.multiple_of(first + 2 * GB, GB)
+        pick(second, odd)
+        add(first, even)
+        pick(third, even)
+        add(second, odd)
+        return c
+
+    lax.fori_loop(0, NG // 2, two, 0)
+    add((NG - 1) * GB, even)
 
 
 def mirror(t, row_mirror, col_mirror):
@@ -388,7 +444,11 @@
         out_shape=jax.ShapeDtypeStruct((ROWS, SLAB), BF),
         in_specs=[pl.BlockSpec(memory_space=pltpu.SMEM), vmem, vmem],
         out_specs=vmem,
-        scratch_shapes=[pltpu.VMEM((SLAB, ROWS), F32), pltpu.VMEM((GB, ROWS), F32)],
+        scratch_shapes=[
+            pltpu.VMEM((SLAB, ROWS), F32),
+            pltpu.VMEM((GB, ROWS), F32),
+            pltpu.VMEM((GB, ROWS), F32),
+        ],
         compiler_params=pltpu.CompilerParams(vmem_limit_bytes=32 * 1024 * 1024),
         name="mirror",
     )(col_mirror, t, row_mirror)

time: 262 us -> 166 us (0.63)
  Pallas kernels: 258 us -> 164 us
    pallas_call x1, Pallas kernels: 237 us -> 151 us  [ladder(): pl.pallas_call(ladder_kernel, out_shape=(jax.ShapeDtypeStruct((SLAB, ROWS...]
    pallas_call x1, Pallas kernels: 21.2 us -> 13.4 us  [mirror(): pl.pallas_call(mirror_kernel, out_shape=jax.ShapeDtypeStruct((ROWS, SLAB)...]
where the time goes in v2:
time: 166 us
  Pallas kernels  164 us (99%)
  local copies, waits for them, and re-layouts  1.69 us (1%)
    pallas_call x1, Pallas kernels, ladder(): pl.pallas_call(ladder_kernel, out_shape=(jax.ShapeDtypeStruct((SLAB, ROWS...  151 us
    pallas_call x1, Pallas kernels, mirror(): pl.pallas_call(mirror_kernel, out_shape=jax.ShapeDtypeStruct((ROWS, SLAB)...  13.4 us

profile of v2, /device:TPU:0, one launch (start us, length us, event | category | flops | bytes accessed | tf_op | source)
XLA Modules:
  0.0 165.8 jit_solution(10641158366055686426)
XLA Ops:
  0.0 0.0 copy-start.1
  0.0 0.0 copy-start.2
  0.0 150.6 %ladder.1 = (bf16[9600,128]{1,0:T(8,128)(2,1)}, bf16[16,128,3072]{2,1,0:T(8,128)(2,1)}, bf16[8,600,3072]{2,1,0:T(8,128)(2,1)}) custom-call(bf16[128,3072]{1,0:T(8,128)(2,1)} %amp_ref.1, bf16[600,3072]{1,0:T(8,128)(2,1)} %bitcast.6, s32[1,128]{1,0:T(1,128)} %bitcast.7), custom_call_target="tpu_custom_call" | custom-call | tf_op jit(solution)/shard_map/ladder/pallas_call | solution.py:357
  150.7 0.0 copy-done.1
  150.7 0.0 copy-done.2
  150.7 0.0 copy-start
  150.7 1.7 %copy-done = bf16[9600,128]{1,0:T(8,128)(2,1)S(1)} copy-done((bf16[9600,128]{1,0:T(8,128)(2,1)S(1)}, bf16[9600,128]{1,0:T(8,128)(2,1)}, u32[]{:S(2)}) %copy-start) | copy-done | bytes 2457624
  152.4 13.4 %mirror.1 = bf16[128,9600]{1,0:T(8,128)(2,1)} custom-call(s32[9600]{0:T(1024)S(1)} %copy-done.1, bf16[9600,128]{1,0:T(8,128)(2,1)S(1)} %copy-done, s32[1,128]{1,0:T(1,128)S(1)} %bitcast.5), custom_call_target="tpu_custom_call" | custom-call | tf_op jit(solution)/shard_map/mirror/pallas_call | solution.py:442
Async XLA Ops:
  0.0 150.7 %copy-start.1 = (s32[9600]{0:T(1024)S(1)}, s32[9600]{0:T(1024)}, u32[]{:S(2)}) copy-start(s32[9600]{0:T(1024)} %col_ref.1) | copy-start | bytes 115204
  0.0 150.7 %copy-start.2 = (s32[128]{0:T(128)S(1)}, s32[128]{0:T(128)}, u32[]{:S(2)}) copy-start(s32[128]{0:T(128)} %param.8) | copy-start | bytes 1540
  150.7 1.7 %copy-start = (bf16[9600,128]{1,0:T(8,128)(2,1)S(1)}, bf16[9600,128]{1,0:T(8,128)(2,1)}, u32[]{:S(2)}) copy-start(bf16[9600,128]{1,0:T(8,128)(2,1)} %get-tuple-element.6.t_ref) | copy-start | bytes 7372804

commit v3 on v2

--- a/solution.py
+++ b/solution.py
@@ -55,25 +55,31 @@
             src_ref=src, dst_ref=dst, send_sem=send, recv_sem=recv, device_id=where, device_id_type=MESH
         )
 
+    def held(j, n, k=None):
+        if j >= CHUNKS[-1][0]:
+            rows = pl.ds(STARTS[j] - STARTS[CHUNKS[-1][0]], PIECES[j])
+            return wlast.at[n, rows] if k is None else wlast.at[n, rows, k]
+        rows = pl.ds(STARTS[j], PIECES[j])
+        return w_all.at[n, rows] if k is None else w_all.at[n, rows, k]
+
     def zop(j, name):
-        rows = pl.ds(STARTS[j], PIECES[j])
+        own = w_ref.at[pl.ds(STARTS[j], PIECES[j])]
         if name == "plus":
-            return remote(w_ref.at[rows], w_all.at[4, rows], ws.at[j, 4], wr.at[j, 4], line(1))
+            return remote(own, held(j, 4), ws.at[j, 4], wr.at[j, 4], line(1))
         if name == "minus":
-            return remote(w_ref.at[rows], w_all.at[2, rows], ws.at[j, 2], wr.at[j, 2], line(3))
+            return remote(own, held(j, 2), ws.at[j, 2], wr.at[j, 2], line(3))
         if name == "far0":
             k = pl.ds(0, HALF)
-            return remote(w_all.at[4, rows, k], w_all.at[6, rows, k], ws.at[j, 6], wr.at[j, 6], line(1))
+            return remote(held(j, 4, k), held(j, 6, k), ws.at[j, 6], wr.at[j, 6], line(1))
         if name == "far1":
             k = pl.ds(HALF, HALF)
-            return remote(w_all.at[2, rows, k], w_all.at[6, rows, k], ws.at[j, 0], wr.at[j, 0], line(3))
+            return remote(held(j, 2, k), held(j, 6, k), ws.at[j, 0], wr.at[j, 0], line(3))
+        if name == "sib0":
+            return remote(own, held(j, 1), ws.at[j, 1], wr.at[j, 1], sibling)
         slot = {"sib2": 2, "sib4": 4, "sib6": 6}[name]
         return remote(
-            w_all.at[slot, rows], w_all.at[slot + 1, rows], ws.at[j, slot + 1], wr.at[j, slot + 1], sibling
+            held(j, slot), held(j, slot + 1), ws.at[j, slot + 1], wr.at[j, slot + 1], sibling
         )
-
-    def sibown():
-        return remote(w_ref, w_all.at[1], ws.at[0, 1], wr.at[0, 1], sibling)
 
     def slot(h, d1, d2):
         return d2 * 4 + d1 if h == 0 else d1 * 4 + d2
@@ -134,7 +140,8 @@
         for h in range(2):
             rop(h, phase, 0).start()
             rop(h, phase, 1).start()
-    sibown().start()
+    for j in range(NP):
+        zop(j, "sib0").start()
 
     irr = irr_ref[...]
     onehot = (lax.broadcasted_iota(jnp.int32, (IRREPS, ROWS), 0) == irr).astype(F32)
@@ -204,31 +211,38 @@
     lax.fori_loop(1, NB, wait_pos, 0)
 
     def wload(j, n):
-        if j < CHUNKS[-1][0]:
+        src = w_ref if n == 0 else w_all.at[n]
+        if j >= CHUNKS[-1][0]:
+            there = held(j, n)
+        else:
             there = wbuf.at[n, pl.ds(128 * (j % 2), PIECES[j])]
-        else:
-            there = wlast.at[n, pl.ds(STARTS[j] - STARTS[CHUNKS[-1][0]], PIECES[j])]
-        src = w_ref if n == 0 else w_all.at[n]
         return pltpu.make_async_copy(src.at[pl.ds(STARTS[j], PIECES[j])], there, wl.at[j, n])
+
+    def loaded(c, n):
+        return c < NC - 1 or n == 0
 
     def near(c):
         for j in CHUNKS[c]:
-            if j == 0:
-                sibown().wait_recv()
+            zop(j, "sib0").wait_recv()
             zop(j, "sib2").wait_recv()
             zop(j, "sib4").wait_recv()
             for n in range(6):
-                wload(j, n).start()
+                if loaded(c, n):
+                    wload(j, n).start()
 
     def far(c):
         for j in CHUNKS[c]:
             zop(j, "far0").wait_recv()
             zop(j, "far1").wait_recv()
             zop(j, "sib6").start()
-            wload(j, 6).start()
+            if loaded(c, 6):
+                wload(j, 6).start()
+
+    def farther(c):
         for j in CHUNKS[c]:
             zop(j, "sib6").wait_recv()
-            wload(j, 7).start()
+            if loaded(c, 7):
+                wload(j, 7).start()
 
     def aload(k):
         return pltpu.make_async_copy(a_all.at[k], abuf.at[k % ABUFS], al.at[k % ABUFS])
@@ -272,7 +286,8 @@
 
         for j in CHUNKS[c]:
             for n in range(first, last):
-                wload(j, n).wait()
+                if loaded(c, n):
+                    wload(j, n).wait()
         lax.fori_loop(first, last, irrep, 0)
 
     def give_back(c):
@@ -310,24 +325,30 @@
         aload(k).start()
     near(0)
     lax.fori_loop(0, NB, sort_block, 0)
+    multiply(0, 0, 6)
+    far(0)
+    multiply(0, 6, 7)
+    farther(0)
+    multiply(0, 7, 8)
+    give_back(0)
     pass_on(3)
     own_chunk(4)
     own_chunk(5)
-    multiply(0, 0, 6)
-    far(0)
-    multiply(0, 6, 8)
     near(1)
-    give_back(0)
     multiply(1, 0, 6)
     far(1)
-    multiply(1, 6, 8)
+    multiply(1, 6, 7)
+    farther(1)
+    multiply(1, 7, 8)
     give_back(1)
     pass_on(4)
     pass_on(5)
     near(2)
-    multiply(2, 0, 6)
+    multiply(2, 0, 4)
     far(2)
-    multiply(2, 6, 8)
+    multiply(2, 4, 7)
+    farther(2)
+    multiply(2, 7, 8)
     give_back(2)
 
     for c in range(NC):
@@ -336,9 +357,8 @@
         pltpu.make_async_copy(some, some, ts.at[c]).wait()
         pltpu.make_async_copy(some, some, tr.at[c]).wait()
     for j in range(NP):
-        for name in ("plus", "minus", "far0", "far1", "sib2", "sib4", "sib6"):
+        for name in ("plus", "minus", "far0", "far1", "sib0", "sib2", "sib4", "sib6"):
             zop(j, name).wait_send()
-    sibown().wait_send()
     for phase in range(5):
         for h in range(2):
             for n in range(4):
@@ -357,12 +377,12 @@
     t, _, _ = pl.pallas_call(
         ladder_kernel,
         out_shape=(
-            jax.ShapeDtypeStruct((SLAB, ROWS), BF),
+            pltpu.VMEM((SLAB, ROWS), BF),
             jax.ShapeDtypeStruct((NB, ROWS, KW), BF),
             jax.ShapeDtypeStruct((IRREPS, COLS, KW), BF),
         ),
         in_specs=[hbm, hbm, pl.BlockSpec(memory_space=pltpu.VMEM)],
-        out_specs=(hbm, hbm, hbm),
+        out_specs=(pl.BlockSpec(memory_space=pltpu.VMEM), hbm, hbm),
         scratch_shapes=[
             pltpu.VMEM((IRREPS, NB * CAP, KW), BF),
             pltpu.VMEM((IRREPS, WIDE, KW), BF),
@@ -387,14 +407,14 @@
             dma((NP, 8)),
         ],
         compiler_params=pltpu.CompilerParams(
-            collective_id=0, has_side_effects=True, vmem_limit_bytes=60 * 1024 * 1024
+            collective_id=0, has_side_effects=True, vmem_limit_bytes=57 * 1024 * 1024
         ),
         name="ladder",
     )(amplitudes, integrals, irreps)
     return t
 
 
-GB = 384
+GB = 1920
 NG = SLAB // GB
 NT = (((1,), (1,)), ((), ()))
 

time: 166 us -> 157 us (0.946)
  Pallas kernels: 164 us -> 156 us
  local copies, waits for them, and re-layouts: 1.69 us -> 0.01 us
    pallas_call x1, Pallas kernels: 151 us -> 145 us  [ladder(): pl.pallas_call(ladder_kernel, out_shape=(pltpu.VMEM((SLAB, ROWS), BF), ja...]
    pallas_call x1, Pallas kernels: 13.4 us -> 11.6 us  [mirror(): pl.pallas_call(mirror_kernel, out_shape=jax.ShapeDtypeStruct((ROWS, SLAB)...]
    unnamed x6 -> x4, local copies, waits for them, and re-layouts: 1.69 us -> 0.01 us
where the time goes in v3:
time: 157 us; the launch traced here: 156 us
  Pallas kernels  156 us (99%)
    pallas_call x1, Pallas kernels, ladder(): pl.pallas_call(ladder_kernel, out_shape=(pltpu.VMEM((SLAB, ROWS), BF), ja...  145 us
    pallas_call x1, Pallas kernels, mirror(): pl.pallas_call(mirror_kernel, out_shape=jax.ShapeDtypeStruct((ROWS, SLAB)...  11.6 us

profile of v3, /device:TPU:0, one launch (start us, length us, event | category | flops | bytes accessed | tf_op | source)
XLA Modules:
  0.0 156.2 jit_solution(18328066144687813992)
XLA Ops:
  0.0 0.0 copy-start
  0.0 0.0 copy-start.1
  0.0 144.6 %ladder.1 = (bf16[9600,128]{1,0:T(8,128)(2,1)S(1)}, bf16[16,128,3072]{2,1,0:T(8,128)(2,1)}, bf16[8,600,3072]{2,1,0:T(8,128)(2,1)}) custom-call(bf16[128,3072]{1,0:T(8,128)(2,1)} %amp_ref.1, bf16[600,3072]{1,0:T(8,128)(2,1)} %bitcast.6, s32[1,128]{1,0:T(1,128)} %bitcast.7), custom_call_target="tpu_custom_call" | custom-call | tf_op jit(solution)/shard_map/ladder/pallas_call | solution.py:377
  144.6 0.0 copy-done
  144.7 0.0 copy-done.1
  144.7 11.6 %mirror.1 = bf16[128,9600]{1,0:T(8,128)(2,1)} custom-call(s32[9600]{0:T(1024)S(1)} %copy-done, bf16[9600,128]{1,0:T(8,128)(2,1)S(1)} %get-tuple-element.6.t_ref, s32[1,128]{1,0:T(1,128)S(1)} %bitcast.5), custom_call_target="tpu_custom_call" | custom-call | tf_op jit(solution)/shard_map/mirror/pallas_call | solution.py:462
Async XLA Ops:
  0.0 144.6 %copy-start = (s32[9600]{0:T(1024)S(1)}, s32[9600]{0:T(1024)}, u32[]{:S(2)}) copy-start(s32[9600]{0:T(1024)} %col_ref.1) | copy-start | bytes 115204
  0.0 144.7 %copy-start.1 = (s32[128]{0:T(128)S(1)}, s32[128]{0:T(128)}, u32[]{:S(2)}) copy-start(s32[128]{0:T(128)} %param.8) | copy-start | bytes 1540
